TPU v7x, 512 devices: a whole 4x8x8 slice. The times are simulated.
512 devices in a mesh: samp: 32 (over x, z), blk: 16 (over y, core).
Axes of the slice: x: 4, y: 8, z: 8, core: 2. Of those that a mesh axis runs over, the one named last changes fastest.
Arguments:
- dosages: int32 [49152, 8192], P('samp', 'blk'), may hold values from 0 to 2, as said below
- new_dosages: int32 [49152, 2048], P('samp', 'blk'), may hold values from 0 to 2, as said below
- traits: float32 [64, 49152], P(None, 'samp'), may hold values from -40 to 40
- shrink: float32 [5], replicated, may hold values from 0.5 to 5
Outputs:
- residual: float32 [5, 64, 49152], P(None, 'blk', 'samp')
- scores: float32 [5, 64, 2048], P(None, None, 'blk')
Inputs may be any that keep to these rules, and one draw needn't show every extreme that they name: `dosages`: codes of haplotype pairs, with linkage along neighbouring variants. `new_dosages`: codes of haplotype pairs, with linkage along neighbouring variants.
All inputs are finite; a program needn't handle non-finite values.
Results may differ from a plain program's by a relative error of at most 0.0053.
Values may be sent and summed in bfloat16 or wider, within the bound.
No kernel may reach another device: no remote copies, remote signals or barrier semaphores. Data moves between devices by JAX's collectives and lax.ppermute only.
A program may use at most 64 MiB of HBM per device.

v0:
```python
import jax
import jax.numpy as jnp
from jax import lax
from jax.sharding import Mesh, PartitionSpec as P

RIDGE = 5
SAMP = ("x", "z")
BLK = ("y", "core")
FACTORS = {32: (4, 8), 16: (8, 2), 4: (2, 2)}
EPS = 1e-05
F32 = jnp.float32
BF16 = jnp.bfloat16


def dot(a, b, contract, precision=None):
    return lax.dot_general(
        a, b, (contract, ((), ())), precision=precision, preferred_element_type=F32
    )


def rounded(values):
    return lax.reduce_precision(values, 8, 7)


def column_stats(shifted_sum, shifted_sq, count):
    mean = (shifted_sum + count) / count
    var = (shifted_sq + 2.0 * shifted_sum + count) / count - mean * mean
    return (mean, 1.0 / jnp.sqrt(var + EPS))


def scaled(codes, mean, inv):
    return ((codes.astype(F32) - mean) * inv).astype(BF16)


def affine(shifted_sum, shifted_sq, mean, inv, count):
    low, mid, high = (rounded((code - mean) * inv) for code in (0.0, 1.0, 2.0))
    n_low = (shifted_sq - shifted_sum) * 0.5
    n_high = (shifted_sq + shifted_sum) * 0.5
    n_mid = count - shifted_sq
    value_mean = (n_low * low + n_mid * mid + n_high * high) / count
    pairs = n_low * n_mid + n_mid * n_high + 4.0 * n_low * n_high
    slopes = (
        n_low * n_mid * (mid - low)
        + n_mid * n_high * (high - mid)
        + 2.0 * n_low * n_high * (high - low)
    )
    slope = jnp.where(pairs > 0.0, slopes / jnp.maximum(pairs, 1.0), inv)
    square = (n_low * low * low + n_mid * mid * mid + n_high * high * high) / count
    return (value_mean, slope, square)


def chebyshev_coefficients(lam, bound):
    centre = lam + bound / 2.0
    half = bound / 2.0
    sig = centre / half
    q0 = 1.0 / sig
    d0 = 1.0 / centre
    r1a, r1b = (1.0 - lam * d0, -d0)
    q1 = 1.0 / (2.0 * sig - q0)
    step = 2.0 * q1 / half
    d1a, d1b = (q1 * q0 * d0 + step * r1a, step * r1b)
    r2a = r1a - lam * d1a
    r2b = r1b - d1a - lam * d1b
    r2c = -d1b
    q2 = 1.0 / (2.0 * sig - q1)
    step = 2.0 * q2 / half
    d2a, d2b, d2c = (q2 * q1 * d1a + step * r2a, q2 * q1 * d1b + step * r2b, step * r2c)
    return (d0 + d1a + d2a, d1b + d2b, d2c)


def shards(dosages, new_dosages, traits, shrink):
    rows, width = dosages.shape
    fresh_width = new_dosages.shape[1]
    trait_count = traits.shape[0]
    samp, blk = (lax.axis_size(SAMP), lax.axis_size(BLK))
    depth, cores, zs = (lax.axis_size("y"), lax.axis_size("core"), lax.axis_size("z"))
    count = float(rows * samp)
    half_width = width // 2
    share_rows = half_width // samp
    share = trait_count // blk
    columns = RIDGE * trait_count
    codes = (dosages - 1).astype(BF16)
    codes_f = (dosages - 1).astype(F32)
    new_f = (new_dosages - 1).astype(F32)
    trait_bf = traits.astype(BF16)
    parts = (
        jnp.sum(codes_f, axis=0),
        jnp.sum(codes_f * codes_f, axis=0),
        jnp.sum(new_f, axis=0),
        jnp.sum(new_f * new_f, axis=0),
        jnp.sum(trait_bf.astype(F32), axis=1),
    )
    sizes = [p.shape[0] for p in parts]
    slots = share_rows * 256
    sums = jnp.pad(jnp.concatenate(parts), (0, slots - sum(sizes))).reshape(share_rows, 256)
    first, second = (codes[:, :half_width], codes[:, half_width:])
    over_rows = ((0,), (0,))
    gram_top = dot(first, codes, over_rows)
    gram_low = dot(second, second, over_rows)
    cross = dot(codes, trait_bf, ((0,), (1,)))
    wide = 3 * half_width
    payload = jnp.concatenate(
        [gram_top, gram_low, cross[:half_width], cross[half_width:]], axis=1
    ).reshape(samp, share_rows, wide + 2 * trait_count)
    payload = jnp.concatenate(
        [payload, jnp.broadcast_to(sums[None], (samp, share_rows, 256))], axis=2
    )
    chunk = jnp.sum(lax.all_to_all(payload, SAMP, 0, 0, tiled=True), axis=0)
    totals = chunk[:, wide + 2 * trait_count :].reshape(slots)
    pieces, at = ([], 0)
    for size in sizes:
        pieces.append(totals[at : at + size])
        at += size
    code_sum, code_sq, new_sum, new_sq, trait_sum = pieces
    mean, inv = column_stats(code_sum, code_sq, count)
    value_mean, slope, square = affine(code_sum, code_sq, mean, inv, count)
    start = lax.axis_index(SAMP) * share_rows

    def own(vector, offset):
        return lax.dynamic_slice(vector, (start + offset,), (share_rows,))[:, None]

    def centred(product, offset, column_from):
        sums_i, slope_i, value_i = (own(v, offset) for v in (code_sum, slope, value_mean))
        out = (
            slope_i
            * slope[None, column_from:]
            * (product / count - sums_i / count * (code_sum[None, column_from:] / count))
        )
        out = out + value_i * value_mean[None, column_from:]
        row = start + offset + lax.broadcasted_iota(jnp.int32, out.shape, 0)
        column = column_from + lax.broadcasted_iota(jnp.int32, out.shape, 1)
        return jnp.where(row == column, 0.0, out)

    def centred_cross(product, offset):
        sums_i, slope_i, value_i = (own(v, offset) for v in (code_sum, slope, value_mean))
        trait_mean = trait_sum[None, :] / count
        return slope_i * (product / count - sums_i / count * trait_mean) + value_i * trait_mean

    rhs_rows = jnp.concatenate(
        [
            centred_cross(chunk[:, wide : wide + trait_count], 0),
            centred_cross(chunk[:, wide + trait_count : wide + 2 * trait_count], half_width),
        ],
        axis=1,
    )
    rhs_high = rounded(rhs_rows)
    own_rows = jnp.concatenate(
        [
            centred(chunk[:, :width], 0, 0),
            centred(chunk[:, width:wide], half_width, half_width),
            rhs_high,
            rhs_rows - rhs_high,
        ],
        axis=1,
    ).astype(BF16)
    every = lax.all_to_all(
        jnp.broadcast_to(own_rows[None], (samp, *own_rows.shape)), SAMP, 0, 0, tiled=True
    ).reshape(half_width, own_rows.shape[1])
    top_left, top_right = (every[:, :half_width], every[:, half_width:width])
    low_right = every[:, width:wide]
    gram = jnp.concatenate(
        [
            jnp.concatenate([top_left, top_right], axis=1),
            jnp.concatenate([top_right.T, low_right], axis=1),
        ],
        axis=0,
    )
    bound = jnp.max(jnp.sum(jnp.abs(gram.astype(F32)), axis=0) + square)
    rhs_parts = every[:, wide:].reshape(half_width, 2, 2, trait_count)
    rhs_parts = rhs_parts.transpose(1, 3, 2, 0).reshape(2 * trait_count, width)

    def apply_gram(high, low, whole):
        out = dot(jnp.concatenate([high, low], axis=0), gram, ((1,), (0,)))
        return out[:trait_count] + out[trait_count:] + square[None, :] * whole

    high, low = (rhs_parts[:trait_count], rhs_parts[trait_count:])
    rhs = high.astype(F32) + low.astype(F32)
    once = apply_gram(high, low, rhs)
    once_high = rounded(once)
    twice = apply_gram(once_high.astype(BF16), (once - once_high).astype(BF16), once)
    coefficients = chebyshev_coefficients(shrink, bound)
    row = lax.broadcasted_iota(jnp.int32, (columns, 3 * trait_count), 0)
    column = lax.broadcasted_iota(jnp.int32, (columns, 3 * trait_count), 1)
    side, in_side = (row // (columns // cores), row % (columns // cores))
    place, in_place = (in_side // (RIDGE * share), in_side % (RIDGE * share))
    ridge, in_share = (in_place // share, in_place % share)
    core = lax.rem(lax.axis_index("core") + 1 + side, cores)
    trait = (place * cores + core) * share + in_share
    mixing = jnp.zeros((columns, 3 * trait_count), F32)
    for power in range(3):
        for r in range(RIDGE):
            mixing = jnp.where(
                (ridge == r) & (column == trait + power * trait_count),
                coefficients[power][r],
                mixing,
            )
    weights = dot(
        mixing, jnp.concatenate([rhs, once, twice], axis=0), ((1,), (0,)), lax.Precision.HIGHEST
    ).astype(BF16)
    standard = scaled(dosages, mean, inv)
    new_mean, new_inv = column_stats(new_sum, new_sq, count)
    fresh = scaled(new_dosages, new_mean, new_inv)
    half_columns = columns // cores
    along = ((1,), (1,))
    sent = dot(weights[:half_columns], standard, along).astype(BF16)
    kept = dot(weights[half_columns:], standard, along)
    arrived = lax.ppermute(sent, "core", [(0, 1), (1, 0)])
    paired = (kept + arrived.astype(F32)).astype(BF16).reshape(depth, RIDGE * share, rows)
    summed = lax.all_to_all(paired, "y", 0, 0, tiled=True)
    pred = jnp.sum(summed.astype(F32), axis=0).reshape(RIDGE, share, rows)
    own_traits = lax.dynamic_slice_in_dim(traits, lax.axis_index(BLK) * share, share, 0)
    residual = own_traits[None] - pred
    res_bf = lax.all_gather(
        residual.astype(BF16).reshape(RIDGE * share, rows), BLK, axis=0, tiled=True
    )
    raw_part = dot(res_bf, fresh, ((1,), (0,)))
    res_float = res_bf.astype(F32)
    squares = jnp.sum(res_float * res_float, axis=1).reshape(zs, 1, columns // zs)
    squares = jnp.pad(squares, ((0, 0), (0, 7), (0, fresh_width - columns // zs)))
    ends = jnp.concatenate([raw_part.reshape(zs, columns // zs, fresh_width), squares], axis=1)
    ends = jnp.sum(lax.all_to_all(ends, "z", 0, 0, tiled=True), axis=0)
    ends = lax.psum(ends, "x")
    raw, sum_sq = (ends[: columns // zs], ends[columns // zs, : columns // zs])
    scores = raw / jnp.sqrt(count * (sum_sq / count + EPS))[:, None]
    scores = lax.all_to_all(
        jnp.broadcast_to(scores[None], (zs, *scores.shape)), "z", 0, 0, tiled=True
    )
    scores = scores.reshape(blk, RIDGE, share, fresh_width).transpose(1, 0, 2, 3)
    return (residual, scores.reshape(RIDGE, trait_count, fresh_width))


def solution(mesh):
    samp, blk = (FACTORS[mesh.shape["samp"]], FACTORS[mesh.shape["blk"]])
    grid = Mesh(mesh.devices.reshape(*samp, *blk), SAMP + BLK)
    return jax.shard_map(
        shards,
        mesh=grid,
        in_specs=(P(SAMP, BLK), P(SAMP, BLK), P(None, SAMP), P()),
        out_specs=(P(None, BLK, SAMP), P(None, None, BLK)),
        check_vma=False,
    )
```

profile of v0, /device:TPU:8, one launch (start us, length us, event | category | flops | bytes accessed | tf_op | source)
XLA Modules:
  0.0 220.9 jit_solution(13262179598304185275)
XLA Ops:
  0.6 2.3 %add_convert_fusion = bf16[1536,512]{1,0:T(8,128)(2,1)S(1)} fusion(s32[1536,512]{1,0:T(8,128)} %param.4), kind=kLoop, calls=%fused_computation.3 | loop fusion | flops 1572864 | bytes 4718592 | tf_op jit(solution)/shard_map/convert_element_type | solution.py:82
  3.0 1.4 fusion.2
  6.6 2.1 fusion.119
  9.8 1.3 constant_dynamic-update-slice_fusion.4
  11.1 1.3 constant_dynamic-update-slice_fusion.3
  13.6 1.3 constant_dynamic-update-slice_fusion.1
  14.9 1.3 constant_dynamic-update-slice_fusion
  16.9 1.4 maximum_bitcast_fusion
  19.4 13.3 %all-to-all-start = ((f32[32,8,1152]{2,1,0:T(8,128)}), f32[32,8,1152]{2,1,0:T(8,128)}, u32[]{:S(2)}, u32[]{:S(2)}) async-start(f32[32,8,1152]{2,1,0:T(8,128)} %pad_maximum_fusion), calls=%async_computation | async-start | bytes 2359296 | tf_op jit(solution)/shard_map/all_to_all | solution.py:108
  33.7 30.3 %all-to-all-done = f32[32,8,1152]{2,1,0:T(8,128)} async-done(((f32[32,8,1152]{2,1,0:T(8,128)}), f32[32,8,1152]{2,1,0:T(8,128)}, u32[]{:S(2)}, u32[]{:S(2)}) %all-to-all-start) | async-done | bytes 1179680 | tf_op jit(solution)/shard_map/all_to_all | solution.py:108
  64.0 2.0 reduce_sum.97
  71.6 5.3 %all-to-all-start.1 = ((bf16[32,8,1024]{2,1,0:T(8,128)(2,1)}), bf16[32,8,1024]{2,1,0:T(8,128)(2,1)}, u32[]{:S(2)}, u32[]{:S(2)}) async-start(bf16[32,8,1024]{2,1,0:T(8,128)(2,1)} %broadcast_in_dim.108), calls=%async_computation.1 | async-start | bytes 1048576 | tf_op jit(solution)/shard_map/all_to_all | solution.py:156
  78.7 14.7 %all-to-all-done.1 = bf16[32,8,1024]{2,1,0:T(8,128)(2,1)} async-done(((bf16[32,8,1024]{2,1,0:T(8,128)(2,1)}), bf16[32,8,1024]{2,1,0:T(8,128)(2,1)}, u32[]{:S(2)}, u32[]{:S(2)}) %all-to-all-start.1) | async-done | bytes 524320 | tf_op jit(solution)/shard_map/all_to_all | solution.py:156
  93.5 1.8 fusion.170
  95.3 1.7 concatenate.57
  96.9 1.7 copy.34
  100.4 1.4 fusion.150
  105.7 1.7 copy.28
  108.5 1.3 fusion.111
  110.6 11.3 %convolution_convert_fusion.1 = bf16[320,512]{1,0:T(8,128)(2,1)S(1)} fusion(f32[64,512]{1,0:T(8,128)S(1)} %fusion.109, f32[64,512]{1,0:T(8,128)S(1)} %get-tuple-element.14, f32[64,512]{1,0:T(8,128)S(1)} %get-tuple-element.20, f32[]{:T(128)} %bitcast.18, f32[]{:T(128)} %bitcast.17, f32[]{:T(128)} %bitcast.16, f32[]{:T(128)} %bitcast.15, f32[]{:T(128)} %bitcast.14, ...), kind=kOutput, calls=%fused_computation.6 | convolution fusion | flops 383008768 | bytes 726720 | tf_op jit(solution)/shard_map/dot_general | solution.py:16
  122.5 1.9 collective-permute-start
  124.5 1.8 collective-permute-done
  126.3 1.5 add_convert_fusion.1
  127.8 2.0 reshape.255
  129.8 7.5 %all-to-all-start.2 = ((bf16[8,20,1536]{2,1,0:T(8,128)(2,1)}), bf16[8,20,1536]{2,1,0:T(8,128)(2,1)S(1)}, u32[]{:S(2)}, u32[]{:S(2)}) async-start(bf16[8,20,1536]{2,1,0:T(8,128)(2,1)} %reshape.255), calls=%async_computation.2 | async-start | bytes 1179648 | tf_op jit(solution)/shard_map/all_to_all | solution.py:209
  138.1 16.9 %all-to-all-done.2 = bf16[8,20,1536]{2,1,0:T(8,128)(2,1)S(1)} async-done(((bf16[8,20,1536]{2,1,0:T(8,128)(2,1)}), bf16[8,20,1536]{2,1,0:T(8,128)(2,1)S(1)}, u32[]{:S(2)}, u32[]{:S(2)}) %all-to-all-start.2) | async-done | bytes 491552 | tf_op jit(solution)/shard_map/all_to_all | solution.py:209
  155.2 19.1 %all-gather = bf16[16,20,1536]{2,1,0:T(8,128)(2,1)S(1)} all-gather(bf16[1,20,1536]{2,1,0:T(8,128)(2,1)S(1)} %fusion.121), channel_id=1, replica_groups=mesh['x'=4,'z'=8,'y'=8,'core'=2] {'y','core'}, dimensions={0}, use_global_device_ids=true | all-gather | bytes 1044480 | tf_op jit(solution)/shard_map/all_gather | solution.py:213
  176.0 4.2 %all-to-all-start.3 = ((f32[8,48,128]{2,1,0:T(8,128)}), f32[8,48,128]{2,1,0:T(8,128)S(1)}, u32[]{:S(2)}, u32[]{:S(2)}) async-start(f32[8,48,128]{2,1,0:T(8,128)} %select_maximum_fusion), calls=%async_computation.3 | async-start | bytes 393216 | tf_op jit(solution)/shard_map/all_to_all | solution.py:221
  180.3 11.0 %all-to-all-done.3 = f32[8,48,128]{2,1,0:T(8,128)S(1)} async-done(((f32[8,48,128]{2,1,0:T(8,128)}), f32[8,48,128]{2,1,0:T(8,128)S(1)}, u32[]{:S(2)}, u32[]{:S(2)}) %all-to-all-start.3) | async-done | bytes 196640 | tf_op jit(solution)/shard_map/all_to_all | solution.py:221
  191.3 15.4 %psum.7 = f32[48,128]{1,0:T(8,128)S(1)} all-reduce(f32[48,128]{1,0:T(8,128)S(1)} %reduce_sum.102), channel_id=1, replica_groups=mesh['x'=4,'z'=8,'y'=8,'core'=2] {'x'}, use_global_device_ids=true, to_apply=%region_11.12 | all-reduce | flops 6144 | bytes 49152 | tf_op jit(solution)/shard_map/psum | solution.py:222
  207.4 3.4 %all-to-all-start.4 = ((f32[8,40,128]{2,1,0:T(8,128)}), f32[8,40,128]{2,1,0:T(8,128)S(1)}, u32[]{:S(2)}, u32[]{:S(2)}) async-start(f32[8,40,128]{2,1,0:T(8,128)} %broadcast_in_dim.125), calls=%async_computation.4 | async-start | bytes 327680 | tf_op jit(solution)/shard_map/all_to_all | solution.py:225
  211.5 8.7 %all-to-all-done.4 = f32[8,40,128]{2,1,0:T(8,128)S(1)} async-done(((f32[8,40,128]{2,1,0:T(8,128)}), f32[8,40,128]{2,1,0:T(8,128)S(1)}, u32[]{:S(2)}, u32[]{:S(2)}) %all-to-all-start.4) | async-done | bytes 163872 | tf_op jit(solution)/shard_map/all_to_all | solution.py:225
  (99 shorter events, 27.3 us)
Async XLA Ops:
  3.0 2.5 %copy-start.1 = (bf16[1536,512]{1,0:T(8,128)(2,1)}, bf16[1536,512]{1,0:T(8,128)(2,1)S(1)}, u32[]{:S(2)}) copy-start(bf16[1536,512]{1,0:T(8,128)(2,1)S(1)} %add_convert_fusion) | copy-start | bytes 4718596
  3.0 2.6 %copy-start = (s32[1536,512]{1,0:T(8,128)S(1)}, s32[1536,512]{1,0:T(8,128)}, u32[]{:S(2)}) copy-start(s32[1536,512]{1,0:T(8,128)} %param.4) | copy-start | bytes 9437188
  5.6 1.0 copy-start.4
  6.6 2.9 %copy-start.2 = (s32[1536,128]{1,0:T(8,128)S(1)}, s32[1536,128]{1,0:T(8,128)}, u32[]{:S(2)}) copy-start(s32[1536,128]{1,0:T(8,128)} %param.5) | copy-start | bytes 2359300
  19.4 44.6 %all-to-all-start = ((f32[32,8,1152]{2,1,0:T(8,128)}), f32[32,8,1152]{2,1,0:T(8,128)}, u32[]{:S(2)}, u32[]{:S(2)}) async-start(f32[32,8,1152]{2,1,0:T(8,128)} %pad_maximum_fusion), calls=%async_computation | async-start | bytes 2359296 | tf_op jit(solution)/shard_map/all_to_all | solution.py:108
  68.5 0.6 copy-start.8
  71.6 21.8 %all-to-all-start.1 = ((bf16[32,8,1024]{2,1,0:T(8,128)(2,1)}), bf16[32,8,1024]{2,1,0:T(8,128)(2,1)}, u32[]{:S(2)}, u32[]{:S(2)}) async-start(bf16[32,8,1024]{2,1,0:T(8,128)(2,1)} %broadcast_in_dim.108), calls=%async_computation.1 | async-start | bytes 1048576 | tf_op jit(solution)/shard_map/all_to_all | solution.py:156
  107.4 2.6 %copy-start.5 = (bf16[256,512]{1,0:T(8,128)(2,1)S(1)}, bf16[256,512]{1,0:T(8,128)(2,1)}, u32[]{:S(2)}) copy-start(bf16[256,512]{1,0:T(8,128)(2,1)} %concatenate.57) | copy-start | bytes 786436
  107.4 2.6 %copy-start.6 = (bf16[256,256]{0,1:T(8,128)(2,1)S(1)}, bf16[256,256]{0,1:T(8,128)(2,1)}, u32[]{:S(2)}) copy-start(bf16[256,256]{0,1:T(8,128)(2,1)} %copy.34) | copy-start | bytes 393220
  107.4 2.6 %copy-start.7 = (bf16[256,256]{1,0:T(8,128)(2,1)S(1)}, bf16[256,256]{1,0:T(8,128)(2,1)}, u32[]{:S(2)}) copy-start(bf16[256,256]{1,0:T(8,128)(2,1)} %get-tuple-element.17) | copy-start | bytes 393220
  109.8 0.7 copy-start.9
  109.9 0.7 copy-start.10
  109.9 0.7 copy-start.11
  109.9 0.7 copy-start.12
  109.9 0.7 copy-start.13
  109.9 0.7 copy-start.14
  122.5 3.8 %collective-permute-start = (bf16[160,1536]{1,0:T(8,128)(2,1)S(1)}, bf16[160,1536]{1,0:T(8,128)(2,1)S(1)}, u32[]{:S(2)}, u32[]{:S(2)}) collective-permute-start(bf16[160,1536]{1,0:T(8,128)(2,1)S(1)} %convolution_convert_fusion), channel_id=1, source_target_pairs={{0,1},{1,0},{2,3},{3,2},{4,5},{5,4},{6,7},{7,6},{8,9},{9,8},{10,11... | collective-permute-start | bytes 1474568 | tf_op jit(solution)/shard_map/ppermute | solution.py:207
  129.8 25.3 %all-to-all-start.2 = ((bf16[8,20,1536]{2,1,0:T(8,128)(2,1)}), bf16[8,20,1536]{2,1,0:T(8,128)(2,1)S(1)}, u32[]{:S(2)}, u32[]{:S(2)}) async-start(bf16[8,20,1536]{2,1,0:T(8,128)(2,1)} %reshape.255), calls=%async_computation.2 | async-start | bytes 1179648 | tf_op jit(solution)/shard_map/all_to_all | solution.py:209
  155.2 19.7 %copy-start.3 = (s32[1536,128]{1,0:T(8,128)S(1)}, s32[1536,128]{1,0:T(8,128)}, u32[]{:S(2)}) copy-start(s32[1536,128]{1,0:T(8,128)} %param.5) | copy-start | bytes 2359300
  176.0 15.2 %all-to-all-start.3 = ((f32[8,48,128]{2,1,0:T(8,128)}), f32[8,48,128]{2,1,0:T(8,128)S(1)}, u32[]{:S(2)}, u32[]{:S(2)}) async-start(f32[8,48,128]{2,1,0:T(8,128)} %select_maximum_fusion), calls=%async_computation.3 | async-start | bytes 393216 | tf_op jit(solution)/shard_map/all_to_all | solution.py:221
  207.4 12.7 %all-to-all-start.4 = ((f32[8,40,128]{2,1,0:T(8,128)}), f32[8,40,128]{2,1,0:T(8,128)S(1)}, u32[]{:S(2)}, u32[]{:S(2)}) async-start(f32[8,40,128]{2,1,0:T(8,128)} %broadcast_in_dim.125), calls=%async_computation.4 | async-start | bytes 327680 | tf_op jit(solution)/shard_map/all_to_all | solution.py:225
where the time goes:
time: 223 us; the launch traced here: 221 us
  waiting for transfers between devices  83.4 us (37%)
  starting transfers between devices  35.7 us (16%)
  blocking collectives  34.5 us (15%)
  local copies, waits for them, and re-layouts  25.3 us (11%)
  other arithmetic  20.5 us (9%)
  matrix products  20 us (9%)
    all_to_all x1, waiting for transfers between devices, shards(): chunk = jnp.sum(lax.all_to_all(payload, SAMP, 0, 0, tiled=True), axis=0)  30.3 us
    dot_general x9, matrix products, dot(): lax.dot_general(a, b, (contract, ((), ())), precision=precision, preferre...  20 us
    all_gather x1, blocking collectives, shards(): lax.all_gather(residual.astype(BF16).reshape(RIDGE * share, rows), BLK, a...  19.1 us
    all_to_all x1, waiting for transfers between devices, shards(): summed = lax.all_to_all(paired, 'y', 0, 0, tiled=True)  16.9 us
    psum x1, blocking collectives, shards(): ends = lax.psum(ends, 'x')  15.4 us
    all_to_all x1, waiting for transfers between devices, shards(): lax.all_to_all(jnp.broadcast_to(own_rows[None], (samp, *own_rows.shape)),...  14.7 us
    all_to_all x1, starting transfers between devices, shards(): chunk = jnp.sum(lax.all_to_all(payload, SAMP, 0, 0, tiled=True), axis=0)  13.3 us
    all_to_all x1, waiting for transfers between devices, shards(): ends = jnp.sum(lax.all_to_all(ends, 'z', 0, 0, tiled=True), axis=0)  11 us
  transfers between devices with their start and end apart: 6, of which 6 were waited for; matrix products, arithmetic and copies ran while one was open for 2% of the time, Pallas kernels for 0%

commit v1 on v0

--- a/solution.py
+++ b/solution.py
@@ -210,9 +210,9 @@
     pred = jnp.sum(summed.astype(F32), axis=0).reshape(RIDGE, share, rows)
     own_traits = lax.dynamic_slice_in_dim(traits, lax.axis_index(BLK) * share, share, 0)
     residual = own_traits[None] - pred
-    res_bf = lax.all_gather(
-        residual.astype(BF16).reshape(RIDGE * share, rows), BLK, axis=0, tiled=True
-    )
+    own_2 = residual.astype(BF16).reshape(RIDGE * share, rows)
+    outgoing = jnp.stack([own_2] * lax.axis_size(BLK))
+    res_bf = jnp.concatenate(lax.all_to_all(outgoing, BLK, 0, 0), axis=0)
     raw_part = dot(res_bf, fresh, ((1,), (0,)))
     res_float = res_bf.astype(F32)
     squares = jnp.sum(res_float * res_float, axis=1).reshape(zs, 1, columns // zs)

time: 223 us -> 238 us (1.067)
  the two profiles are of different devices: /device:TPU:8 before, /device:TPU:24 now
where the time goes in v1:
time: 238 us; the launch traced here: 236 us
  waiting for transfers between devices  109 us (46%)
  starting transfers between devices  43.3 us (18%)
  local copies, waits for them, and re-layouts  25.7 us (11%)
  other arithmetic  20.6 us (9%)
  matrix products  20 us (8%)
  blocking collectives  15.4 us (6%)
    all_to_all x1, waiting for transfers between devices, shards(): chunk = jnp.sum(lax.all_to_all(payload, SAMP, 0, 0, tiled=True), axis=0)  30.2 us
    all_to_all x1, waiting for transfers between devices, shards(): res_bf = jnp.concatenate(lax.all_to_all(outgoing, BLK, 0, 0), axis=0)  28.3 us
    dot_general x9, matrix products, dot(): lax.dot_general(a, b, (contract, ((), ())), precision=precision, preferre...  20 us
    psum x1, blocking collectives, shards(): ends = lax.psum(ends, 'x')  15.4 us
    all_to_all x1, waiting for transfers between devices, shards(): summed = lax.all_to_all(paired, 'y', 0, 0, tiled=True)  14.9 us
    all_to_all x1, waiting for transfers between devices, shards(): lax.all_to_all(jnp.broadcast_to(own_rows[None], (samp, *own_rows.shape)),...  14.8 us
    all_to_all x1, starting transfers between devices, shards(): chunk = jnp.sum(lax.all_to_all(payload, SAMP, 0, 0, tiled=True), axis=0)  13.3 us
    all_to_all x1, waiting for transfers between devices, shards(): ends = jnp.sum(lax.all_to_all(ends, 'z', 0, 0, tiled=True), axis=0)  10.7 us
  transfers between devices with their start and end apart: 7, of which 7 were waited for; matrix products, arithmetic and copies ran while one was open for 2% of the time, Pallas kernels for 0%

profile of v1, /device:TPU:24, one launch (start us, length us, event | category | flops | bytes accessed | tf_op | source)
XLA Modules:
  0.0 236.1 jit_solution(4615177918906513351)
XLA Ops:
  0.6 2.3 add_convert_fusion
  3.0 1.4 fusion.2
  6.2 2.1 fusion.121
  9.4 1.3 constant_dynamic-update-slice_fusion.4
  10.6 1.3 constant_dynamic-update-slice_fusion.3
  14.5 1.3 constant_dynamic-update-slice_fusion
  16.5 1.4 maximum_bitcast_fusion
  19.0 13.3 %all-to-all-start = ((f32[32,8,1152]{2,1,0:T(8,128)}), f32[32,8,1152]{2,1,0:T(8,128)}, u32[]{:S(2)}, u32[]{:S(2)}) async-start(f32[32,8,1152]{2,1,0:T(8,128)} %pad_maximum_fusion), calls=%async_computation | async-start | bytes 2359296 | tf_op jit(solution)/shard_map/all_to_all | solution.py:108
  33.4 30.2 %all-to-all-done = f32[32,8,1152]{2,1,0:T(8,128)} async-done(((f32[32,8,1152]{2,1,0:T(8,128)}), f32[32,8,1152]{2,1,0:T(8,128)}, u32[]{:S(2)}, u32[]{:S(2)}) %all-to-all-start) | async-done | bytes 1179680 | tf_op jit(solution)/shard_map/all_to_all | solution.py:108
  63.6 2.0 reduce_sum.97
  71.2 5.3 %all-to-all-start.1 = ((bf16[32,8,1024]{2,1,0:T(8,128)(2,1)}), bf16[32,8,1024]{2,1,0:T(8,128)(2,1)}, u32[]{:S(2)}, u32[]{:S(2)}) async-start(bf16[32,8,1024]{2,1,0:T(8,128)(2,1)} %broadcast_in_dim.108), calls=%async_computation.1 | async-start | bytes 1048576 | tf_op jit(solution)/shard_map/all_to_all | solution.py:156
  78.3 14.8 %all-to-all-done.1 = bf16[32,8,1024]{2,1,0:T(8,128)(2,1)} async-done(((bf16[32,8,1024]{2,1,0:T(8,128)(2,1)}), bf16[32,8,1024]{2,1,0:T(8,128)(2,1)}, u32[]{:S(2)}, u32[]{:S(2)}) %all-to-all-start.1) | async-done | bytes 524320 | tf_op jit(solution)/shard_map/all_to_all | solution.py:156
  93.1 1.8 fusion.171
  94.8 1.7 concatenate.57
  96.5 1.7 copy.26
  100.0 1.5 fusion.151
  105.5 1.7 copy.20
  108.3 1.3 fusion.113
  110.1 11.3 %convolution_convert_fusion.1 = bf16[320,512]{1,0:T(8,128)(2,1)S(1)} fusion(f32[64,512]{1,0:T(8,128)S(1)} %fusion.111, f32[64,512]{1,0:T(8,128)S(1)} %get-tuple-element.14, f32[64,512]{1,0:T(8,128)S(1)} %get-tuple-element.20, f32[]{:T(128)} %bitcast.18, f32[]{:T(128)} %bitcast.17, f32[]{:T(128)} %bitcast.16, f32[]{:T(128)} %bitcast.15, f32[]{:T(128)} %bitcast.14, ...), kind=kOutput, calls=%fused_computation.6 | convolution fusion | flops 383008768 | bytes 726720 | tf_op jit(solution)/shard_map/dot_general | solution.py:16
  122.1 1.9 collective-permute-start
  124.0 1.8 collective-permute-done
  125.8 1.5 add_convert_fusion.1
  127.3 2.0 reshape.260
  129.3 7.3 %all-to-all-start.2 = ((bf16[8,20,1536]{2,1,0:T(8,128)(2,1)}), bf16[8,20,1536]{2,1,0:T(8,128)(2,1)S(1)}, u32[]{:S(2)}, u32[]{:S(2)}) async-start(bf16[8,20,1536]{2,1,0:T(8,128)(2,1)} %reshape.260), calls=%async_computation.2 | async-start | bytes 1179648 | tf_op jit(solution)/shard_map/all_to_all | solution.py:209
  136.7 14.9 %all-to-all-done.2 = bf16[8,20,1536]{2,1,0:T(8,128)(2,1)S(1)} async-done(((bf16[8,20,1536]{2,1,0:T(8,128)(2,1)}), bf16[8,20,1536]{2,1,0:T(8,128)(2,1)S(1)}, u32[]{:S(2)}, u32[]{:S(2)}) %all-to-all-start.2) | async-done | bytes 491552 | tf_op jit(solution)/shard_map/all_to_all | solution.py:209
  152.8 7.9 %all-to-all-start.3 = ((bf16[16,20,1536]{2,1,0:T(8,128)(2,1)}), bf16[16,20,1536]{2,1,0:T(8,128)(2,1)S(1)}, u32[]{:S(2)}, u32[]{:S(2)}) async-start(bf16[16,20,1536]{2,1,0:T(8,128)(2,1)} %stack.3), calls=%async_computation.3 | async-start | bytes 2359296 | tf_op jit(solution)/shard_map/all_to_all | solution.py:215
  161.5 28.3 %all-to-all-done.3 = bf16[16,20,1536]{2,1,0:T(8,128)(2,1)S(1)} async-done(((bf16[16,20,1536]{2,1,0:T(8,128)(2,1)}), bf16[16,20,1536]{2,1,0:T(8,128)(2,1)S(1)}, u32[]{:S(2)}, u32[]{:S(2)}) %all-to-all-start.3) | async-done | bytes 983072 | tf_op jit(solution)/shard_map/all_to_all | solution.py:215
  191.5 4.2 %all-to-all-start.4 = ((f32[8,48,128]{2,1,0:T(8,128)}), f32[8,48,128]{2,1,0:T(8,128)S(1)}, u32[]{:S(2)}, u32[]{:S(2)}) async-start(f32[8,48,128]{2,1,0:T(8,128)} %select_maximum_fusion), calls=%async_computation.4 | async-start | bytes 393216 | tf_op jit(solution)/shard_map/all_to_all | solution.py:221
  195.8 10.7 %all-to-all-done.4 = f32[8,48,128]{2,1,0:T(8,128)S(1)} async-done(((f32[8,48,128]{2,1,0:T(8,128)}), f32[8,48,128]{2,1,0:T(8,128)S(1)}, u32[]{:S(2)}, u32[]{:S(2)}) %all-to-all-start.4) | async-done | bytes 196640 | tf_op jit(solution)/shard_map/all_to_all | solution.py:221
  206.5 15.4 %psum.7 = f32[48,128]{1,0:T(8,128)S(1)} all-reduce(f32[48,128]{1,0:T(8,128)S(1)} %reduce_sum.102), channel_id=1, replica_groups=mesh['x'=4,'z'=8,'y'=8,'core'=2] {'x'}, use_global_device_ids=true, to_apply=%region_11.12 | all-reduce | flops 6144 | bytes 49152 | tf_op jit(solution)/shard_map/psum | solution.py:222
  222.7 3.4 %all-to-all-start.5 = ((f32[8,40,128]{2,1,0:T(8,128)}), f32[8,40,128]{2,1,0:T(8,128)S(1)}, u32[]{:S(2)}, u32[]{:S(2)}) async-start(f32[8,40,128]{2,1,0:T(8,128)} %broadcast_in_dim.125), calls=%async_computation.5 | async-start | bytes 327680 | tf_op jit(solution)/shard_map/all_to_all | solution.py:225
  226.8 8.7 %all-to-all-done.5 = f32[8,40,128]{2,1,0:T(8,128)S(1)} async-done(((f32[8,40,128]{2,1,0:T(8,128)}), f32[8,40,128]{2,1,0:T(8,128)S(1)}, u32[]{:S(2)}, u32[]{:S(2)}) %all-to-all-start.5) | async-done | bytes 163872 | tf_op jit(solution)/shard_map/all_to_all | solution.py:225
  (101 shorter events, 29.1 us)
Async XLA Ops:
  3.0 2.5 %copy-start.1 = (bf16[1536,512]{1,0:T(8,128)(2,1)}, bf16[1536,512]{1,0:T(8,128)(2,1)S(1)}, u32[]{:S(2)}) copy-start(bf16[1536,512]{1,0:T(8,128)(2,1)S(1)} %add_convert_fusion) | copy-start | bytes 4718596
  3.0 2.6 %copy-start = (s32[1536,512]{1,0:T(8,128)S(1)}, s32[1536,512]{1,0:T(8,128)}, u32[]{:S(2)}) copy-start(s32[1536,512]{1,0:T(8,128)} %param.4) | copy-start | bytes 9437188
  4.4 1.8 copy-start.4
  6.2 2.9 %copy-start.2 = (s32[1536,128]{1,0:T(8,128)S(1)}, s32[1536,128]{1,0:T(8,128)}, u32[]{:S(2)}) copy-start(s32[1536,128]{1,0:T(8,128)} %param.5) | copy-start | bytes 2359300
  19.0 44.6 %all-to-all-start = ((f32[32,8,1152]{2,1,0:T(8,128)}), f32[32,8,1152]{2,1,0:T(8,128)}, u32[]{:S(2)}, u32[]{:S(2)}) async-start(f32[32,8,1152]{2,1,0:T(8,128)} %pad_maximum_fusion), calls=%async_computation | async-start | bytes 2359296 | tf_op jit(solution)/shard_map/all_to_all | solution.py:108
  68.0 0.6 copy-start.8
  71.2 21.8 %all-to-all-start.1 = ((bf16[32,8,1024]{2,1,0:T(8,128)(2,1)}), bf16[32,8,1024]{2,1,0:T(8,128)(2,1)}, u32[]{:S(2)}, u32[]{:S(2)}) async-start(bf16[32,8,1024]{2,1,0:T(8,128)(2,1)} %broadcast_in_dim.108), calls=%async_computation.1 | async-start | bytes 1048576 | tf_op jit(solution)/shard_map/all_to_all | solution.py:156
  107.1 2.6 %copy-start.5 = (bf16[256,512]{1,0:T(8,128)(2,1)S(1)}, bf16[256,512]{1,0:T(8,128)(2,1)}, u32[]{:S(2)}) copy-start(bf16[256,512]{1,0:T(8,128)(2,1)} %concatenate.57) | copy-start | bytes 786436
  107.1 2.6 %copy-start.6 = (bf16[256,256]{0,1:T(8,128)(2,1)S(1)}, bf16[256,256]{0,1:T(8,128)(2,1)}, u32[]{:S(2)}) copy-start(bf16[256,256]{0,1:T(8,128)(2,1)} %copy.26) | copy-start | bytes 393220
  107.1 2.6 %copy-start.7 = (bf16[256,256]{1,0:T(8,128)(2,1)S(1)}, bf16[256,256]{1,0:T(8,128)(2,1)}, u32[]{:S(2)}) copy-start(bf16[256,256]{1,0:T(8,128)(2,1)} %get-tuple-element.17) | copy-start | bytes 393220
  108.3 1.8 copy-start.9
  108.3 1.8 copy-start.10
  108.3 1.8 copy-start.11
  108.3 1.8 copy-start.12
  108.3 1.8 copy-start.13
  108.3 1.8 copy-start.14
  122.1 3.8 %collective-permute-start = (bf16[160,1536]{1,0:T(8,128)(2,1)S(1)}, bf16[160,1536]{1,0:T(8,128)(2,1)S(1)}, u32[]{:S(2)}, u32[]{:S(2)}) collective-permute-start(bf16[160,1536]{1,0:T(8,128)(2,1)S(1)} %convolution_convert_fusion), channel_id=1, source_target_pairs={{0,1},{1,0},{2,3},{3,2},{4,5},{5,4},{6,7},{7,6},{8,9},{9,8},{10,11... | collective-permute-start | bytes 1474568 | tf_op jit(solution)/shard_map/ppermute | solution.py:207
  129.3 22.3 %all-to-all-start.2 = ((bf16[8,20,1536]{2,1,0:T(8,128)(2,1)}), bf16[8,20,1536]{2,1,0:T(8,128)(2,1)S(1)}, u32[]{:S(2)}, u32[]{:S(2)}) async-start(bf16[8,20,1536]{2,1,0:T(8,128)(2,1)} %reshape.260), calls=%async_computation.2 | async-start | bytes 1179648 | tf_op jit(solution)/shard_map/all_to_all | solution.py:209
  152.8 37.5 %copy-start.3 = (s32[1536,128]{1,0:T(8,128)S(1)}, s32[1536,128]{1,0:T(8,128)}, u32[]{:S(2)}) copy-start(s32[1536,128]{1,0:T(8,128)} %param.5) | copy-start | bytes 2359300
  152.8 36.9 %all-to-all-start.3 = ((bf16[16,20,1536]{2,1,0:T(8,128)(2,1)}), bf16[16,20,1536]{2,1,0:T(8,128)(2,1)S(1)}, u32[]{:S(2)}, u32[]{:S(2)}) async-start(bf16[16,20,1536]{2,1,0:T(8,128)(2,1)} %stack.3), calls=%async_computation.3 | async-start | bytes 2359296 | tf_op jit(solution)/shard_map/all_to_all | solution.py:215
  191.5 15.0 %all-to-all-start.4 = ((f32[8,48,128]{2,1,0:T(8,128)}), f32[8,48,128]{2,1,0:T(8,128)S(1)}, u32[]{:S(2)}, u32[]{:S(2)}) async-start(f32[8,48,128]{2,1,0:T(8,128)} %select_maximum_fusion), calls=%async_computation.4 | async-start | bytes 393216 | tf_op jit(solution)/shard_map/all_to_all | solution.py:221
  222.7 12.7 %all-to-all-start.5 = ((f32[8,40,128]{2,1,0:T(8,128)}), f32[8,40,128]{2,1,0:T(8,128)S(1)}, u32[]{:S(2)}, u32[]{:S(2)}) async-start(f32[8,40,128]{2,1,0:T(8,128)} %broadcast_in_dim.125), calls=%async_computation.5 | async-start | bytes 327680 | tf_op jit(solution)/shard_map/all_to_all | solution.py:225
